TPU v7x, 256 devices: a whole 4x4x8 slice. The times are simulated.
256 devices in a mesh: gx: 4 (over x_lo, core), gy: 16 (over x_hi, z), gz: 4 (over y).
Axes of the slice: x: 4 (x_hi: 2, x_lo: 2; x = x_hi * 2 + x_lo), y: 4, z: 8, core: 2. Of those that a mesh axis runs over, the one named last changes fastest.
Arguments:
- field: bfloat16 [64, 8, 384, 1536], P(None, 'gz', 'gy', 'gx'), may hold values from -200 to 200, as said below
- mode_one_factor: bfloat16 [1536, 256], P('gx'), may hold values from -0.15625 to 0.15625
- mode_two_factor: bfloat16 [384, 256], P('gy'), may hold values from -0.3125 to 0.3125
Outputs:
- gram_one: float32 [1536, 1536], P('gx')
- gram_two: float32 [384, 384], P('gy')
- core: bfloat16 [64, 8, 256, 256], P('gx', 'gz', 'gy')
Inputs may be any that keep to these rules, and one draw needn't show every extreme that they name: `field`: the snapshot's values lie within -200 and 200.
All inputs are finite; a program needn't handle non-finite values.
Results may differ from a plain program's by a relative error of at most 0.005.
Values may be sent and summed in bfloat16 or wider, within the bound.
A program may use at most 128 MiB of HBM per device.

v0:
```python
import jax
import jax.numpy as jnp
from jax import lax
from jax.sharding import PartitionSpec as P


def local(field, mode_one_factor, mode_two_factor):
    vars_all, cells_three, cells_two, cells_one = field.shape
    rank_one = mode_one_factor.shape[1]
    count_gx = lax.axis_size("gx")
    own_rows = vars_all // count_gx
    total_three = cells_three * lax.axis_size("gz")
    total_two = cells_two * lax.axis_size("gy")
    flat_own = field.reshape(-1, cells_one)
    piece = lax.all_gather(field, "gx", axis=3, tiled=True)
    width = piece.shape[3]
    gram_block = lax.dot_general(
        flat_own,
        piece.reshape(-1, width),
        (((0,), (0,)), ((), ())),
        preferred_element_type=jnp.float32,
    )
    product = jnp.dot(
        field.reshape(-1, cells_one), mode_one_factor, preferred_element_type=jnp.float32
    )
    shrunk_sum = lax.psum_scatter(
        product.reshape(own_rows * lax.axis_size("gx"), cells_three, cells_two, rank_one),
        "gx",
        scatter_dimension=0,
        tiled=True,
    )
    gram_one = lax.psum(gram_block, ("gy", "gz")) * (1.0 / (vars_all * total_three * total_two))
    shrunk = shrunk_sum.astype(jnp.bfloat16)
    gram_two_block = jnp.einsum(
        "akjr,akqr->jq",
        shrunk,
        lax.all_gather(shrunk, "gy", axis=2, tiled=True),
        preferred_element_type=jnp.float32,
    )
    partial_core = jnp.einsum(
        "akjr,js->aksr", shrunk, mode_two_factor, preferred_element_type=jnp.float32
    )
    core = lax.psum_scatter(partial_core, "gy", scatter_dimension=2, tiled=True).astype(
        jnp.bfloat16
    )
    gram_two = lax.psum(gram_two_block, ("gx", "gz")) * (1.0 / (vars_all * total_three * rank_one))
    return (gram_one, gram_two, core)


def solution(mesh):
    placed = (P(None, "gz", "gy", "gx"), P("gx", None), P("gy", None))
    return jax.shard_map(
        local,
        mesh=mesh,
        in_specs=placed,
        out_specs=(P("gx", None), P("gy", None), P("gx", "gz", "gy", None)),
        check_vma=False,
    )
```

profile of v0, /device:TPU:8, one launch (start us, length us, event | category | flops | bytes accessed | tf_op | source)
XLA Modules:
  0.0 1197.3 jit_solution(16504379202459117194)
XLA Ops:
  7.2 0.0 copy-start
  7.2 0.0 all-gather.3.cloned.1.call-start
  7.2 3.7 copy.9
  10.9 0.0 all-gather.3.cloned.1.call-update
  10.9 0.0 reduce-scatter.3.cloned.1.call-start
  11.0 0.0 copy-done
  11.0 1.6 copy-done.1
  12.6 2.6 fusion.5
  15.2 0.0 reduce-scatter.3.cloned.1.call-update
  15.2 0.0 all-reduce.2.cloned.1.call-start
  15.3 89.8 %all-gather.3.cloned.1.call-done = bf16[64,2,24,1536]{3,0,2,1:T(8,128)(2,1)} async-done(((bf16[64,2,24,384]{3,0,2,1:T(8,128)(2,1)}), bf16[64,2,24,1536]{3,0,2,1:T(8,128)(2,1)}) %all-gather.3.cloned.1.call-update) | async-done | bytes 9437200 | tf_op jit(solution)/shard_map/all_gather | solution.py:15
  105.1 17.4 %fusion.2 = f32[384,1536]{1,0:T(8,128)} fusion(bf16[64,2,24,384]{3,2,1,0:T(8,128)(2,1)S(1)} %copy-done.1, bf16[64,2,24,1536]{3,0,2,1:T(8,128)(2,1)} %all-gather.3.cloned.1.call-done), kind=kOutput, calls=%fused_computation.3 | convolution fusion | flops 3623878656 | bytes 14155776 | tf_op jit(solution)/shard_map/dot_general | solution.py:17
  122.5 0.0 all-reduce.2.cloned.1.call-update
  122.5 0.0 all-gather.5.cloned.1.call-start
  122.5 26.8 %reduce-scatter.3.cloned.1.call-done = f32[16,2,24,256]{3,2,1,0:T(8,128)} async-done(((f32[64,2,24,256]{3,2,1,0:T(8,128)}), f32[16,2,24,256]{3,2,1,0:T(8,128)}) %reduce-scatter.3.cloned.1.call-update) | async-done | bytes 786448 | tf_op jit(solution)/shard_map/reduce_scatter | solution.py:26
  149.3 2.0 convert_element_type.6
  151.3 0.0 all-gather.5.cloned.1.call-update
  151.3 0.0 reduce-scatter.5.cloned.1.call-start
  151.3 0.0 copy-done.3
  151.4 5.5 convolution_bitcast_fusion
  156.9 10.5 copy.11
  167.4 0.0 reduce-scatter.5.cloned.1.call-update
  167.4 0.0 copy-start.2
  167.4 677.4 %all-reduce.2.cloned.1.call-done = f32[384,1536]{1,0:T(8,128)} async-done(((f32[384,1536]{1,0:T(8,128)}), f32[384,1536]{1,0:T(8,128)}) %all-reduce.2.cloned.1.call-update) | async-done | bytes 2359312 | tf_op jit(solution)/shard_map/psum | solution.py:32
  844.8 3.3 broadcast_multiply_fusion
  848.1 114.3 %all-gather.5.cloned.1.call-done = bf16[16,2,384,256]{3,2,1,0:T(8,128)(2,1)} async-done(((bf16[16,2,24,256]{3,2,1,0:T(8,128)(2,1)}), bf16[16,2,384,256]{3,2,1,0:T(8,128)(2,1)}) %all-gather.5.cloned.1.call-update) | async-done | bytes 6291472 | tf_op jit(solution)/shard_map/all_gather | solution.py:37
  962.4 4.5 convolution_bitcast_fusion.1
  966.9 52.5 %psum.15 = f32[24,384]{1,0:T(8,128)S(1)} all-reduce(f32[24,384]{1,0:T(8,128)S(1)} %convolution_bitcast_fusion.1), channel_id=1, replica_groups=mesh['gx'=4,'gy'=16,'gz'=4] {'gx','gz'}, use_global_device_ids=true, to_apply=%region_2.0 | all-reduce | flops 9216 | bytes 73728 | tf_op jit(solution)/shard_map/psum | solution.py:46
  1019.4 0.6 broadcast_multiply_fusion.1
  1020.0 168.8 %reduce-scatter.5.cloned.1.call-done = f32[16,2,16,256]{3,0,1,2:T(8,128)} async-done(((f32[16,2,256,256]{3,0,1,2:T(8,128)}), f32[16,2,16,256]{3,0,1,2:T(8,128)}) %reduce-scatter.5.cloned.1.call-update) | async-done | bytes 524304 | tf_op jit(solution)/shard_map/reduce_scatter | solution.py:43
  1188.8 1.1 convert_element_type.7
  1189.9 0.9 copy.12
  (3 shorter events, 0.0 us)
Async XLA Ops:
  7.2 3.8 copy-start
  7.2 97.9 %all-gather.3.cloned.1.call-start = ((), (), s32[]{:S(2)}) async-start(), calls=%async_computation.2 | async-start | bytes 11796480 | tf_op jit(solution)/shard_map/all_gather | solution.py:15
  10.9 1.7 copy-start.1
  10.9 138.4 %reduce-scatter.3.cloned.1.call-start = ((), (), s32[]{:S(2)}) async-start(), calls=%async_computation.4 | async-start | bytes 3932160 | tf_op jit(solution)/shard_map/reduce_scatter | solution.py:26
  15.2 829.6 %all-reduce.2.cloned.1.call-start = ((), (), s32[]{:S(2)}) async-start(), calls=%async_computation.3 | async-start | bytes 4718592 | tf_op jit(solution)/shard_map/psum | solution.py:32
  122.5 28.9 %copy-start.3 = (bf16[24,256]{1,0:T(8,128)(2,1)S(1)}, bf16[24,256]{1,0:T(8,128)(2,1)}, u32[]{:S(2)}) copy-start(bf16[24,256]{1,0:T(8,128)(2,1)} %param.5) | copy-start | bytes 36868
  122.5 839.9 %all-gather.5.cloned.1.call-start = ((), (), s32[]{:S(2)}) async-start(), calls=%async_computation.5 | async-start | bytes 6684672 | tf_op jit(solution)/shard_map/all_gather | solution.py:37
  151.3 1037.5 %reduce-scatter.5.cloned.1.call-start = ((), (), s32[]{:S(2)}) async-start(), calls=%async_computation.6 | async-start | bytes 8912896 | tf_op jit(solution)/shard_map/reduce_scatter | solution.py:43
  167.4 795.0 %copy-start.2 = (bf16[16,2,24,256]{3,2,1,0:T(8,128)(2,1)S(1)}, bf16[16,2,24,256]{3,2,1,0:T(8,128)(2,1)}, u32[]{:S(2)}) copy-start(bf16[16,2,24,256]{3,2,1,0:T(8,128)(2,1)} %convert_element_type.6) | copy-start | bytes 1179652
Sparse Core Ops, SparseCore 0:
  11.1 93.9 all-gather.2
  107.6 41.6 reduce-scatter.2
  152.5 692.2 all-reduce.1
  847.3 115.0 all-gather.4
  966.3 222.4 reduce-scatter.4
where the time goes:
time: 1200 us
  waiting for transfers between devices  1080 us (90%)
  blocking collectives  52.5 us (4%)
  matrix products  30.1 us (3%)
  local copies, waits for them, and re-layouts  16.6 us (1%)
  between operations  13.8 us (1%)
    psum x1, waiting for transfers between devices, local(): lax.psum(gram_block, ('gy', 'gz'))  677 us
    reduce_scatter x1, waiting for transfers between devices, local(): lax.psum_scatter(partial_core, 'gy', scatter_dimension=2, tiled=True)  169 us
    all_gather x1, waiting for transfers between devices, local(): lax.all_gather(shrunk, 'gy', axis=2, tiled=True)  114 us
    all_gather x1, waiting for transfers between devices, local(): piece = lax.all_gather(field, 'gx', axis=3, tiled=True)  89.8 us
    psum x1, blocking collectives, local(): lax.psum(gram_two_block, ('gx', 'gz'))  52.5 us
    reduce_scatter x1, waiting for transfers between devices, local(): lax.psum_scatter(product.reshape(own_rows * lax.axis_size('gx'), cells_th...  26.8 us
  transfers between devices with their start and end apart: 5, of which 5 were waited for; matrix products, arithmetic and copies ran while one was open for 4% of the time, Pallas kernels for 0%

commit v1 on v0

--- a/solution.py
+++ b/solution.py
@@ -12,7 +12,9 @@
     total_three = cells_three * lax.axis_size("gz")
     total_two = cells_two * lax.axis_size("gy")
     flat_own = field.reshape(-1, cells_one)
-    piece = lax.all_gather(field, "gx", axis=3, tiled=True)
+    piece = jnp.concatenate(
+        lax.all_to_all(jnp.stack([field] * lax.axis_size("gx")), "gx", 0, 0), axis=3
+    )
     width = piece.shape[3]
     gram_block = lax.dot_general(
         flat_own,

time: 1200 us -> 973 us (0.81)
  waiting for transfers between devices: 1080 us -> 818 us
  local copies, waits for them, and re-layouts: 16.6 us -> 50.2 us
    reduce_scatter x1, waiting for transfers between devices: 169 us -> 0.01 us  [local(): lax.psum_scatter(partial_core, 'gy', scatter_dimension=2, tiled=True)]
    all_to_all x0 -> x1, waiting for transfers between devices: none -> 127 us  [local(): lax.all_to_all(jnp.stack([field] * lax.axis_size('gx')), 'gx', 0, 0)]
    all_gather x1, waiting for transfers between devices: 114 us -> 0.01 us  [local(): lax.all_gather(shrunk, 'gy', axis=2, tiled=True)]
    all_gather x1 -> x0, waiting for transfers between devices: 89.8 us -> none  [local(): piece = lax.all_gather(field, 'gx', axis=3, tiled=True)]
    reduce_scatter x1, waiting for transfers between devices: 26.8 us -> 0.02 us  [local(): lax.psum_scatter(product.reshape(own_rows * lax.axis_size('gx'), cells_th...]
    reshape x0 -> x1, local copies, waits for them, and re-layouts: none -> 23.7 us  [local(): jnp.concatenate(lax.all_to_all(jnp.stack([field] * lax.axis_size('gx')),...]
    psum x1, waiting for transfers between devices: 677 us -> 691 us  [local(): lax.psum(gram_block, ('gy', 'gz'))]
  transfers between devices with their start and end apart: 5 -> 5, of which waited for: 5 -> 2; matrix products, arithmetic and copies ran while one was open for 4% -> 7% of each run, Pallas kernels for 0% -> 0%
where the time goes in v1:
time: 973 us; the launch traced here: 972 us
  waiting for transfers between devices  818 us (84%)
  blocking collectives  55.5 us (6%)
  local copies, waits for them, and re-layouts  50.2 us (5%)
  matrix products  20.5 us (2%)
  between operations  15.3 us (2%)
    psum x1, waiting for transfers between devices, local(): lax.psum(gram_block, ('gy', 'gz'))  691 us
    all_to_all x1, waiting for transfers between devices, local(): lax.all_to_all(jnp.stack([field] * lax.axis_size('gx')), 'gx', 0, 0)  127 us
    psum x1, blocking collectives, local(): lax.psum(gram_two_block, ('gx', 'gz'))  55.5 us
    reshape x1, local copies, waits for them, and re-layouts, local(): jnp.concatenate(lax.all_to_all(jnp.stack([field] * lax.axis_size('gx')),...  23.7 us
  transfers between devices with their start and end apart: 5, of which 2 were waited for; matrix products, arithmetic and copies ran while one was open for 7% of the time, Pallas kernels for 0%

profile of v1, /device:TPU:8, one launch (start us, length us, event | category | flops | bytes accessed | tf_op | source)
XLA Modules:
  0.0 972.4 jit_solution(16921907441099503279)
XLA Ops:
  8.0 0.0 copy-start
  8.0 6.2 stack.2
  14.2 5.9 all-to-all-start
  20.1 0.0 reduce-scatter.3.cloned.1.call-start
  20.2 0.0 copy-done
  20.2 0.0 copy-done.2
  20.2 2.6 fusion
  22.8 0.0 reduce-scatter.3.cloned.1.call-update
  22.9 0.0 all-reduce.2.cloned.1.call-start
  22.9 126.9 %all-to-all-done = bf16[4,64,2,24,384]{4,3,2,1,0:T(8,128)(2,1)} async-done(((bf16[4,64,2,24,384]{4,3,2,1,0:T(8,128)(2,1)}), bf16[4,64,2,24,384]{4,3,2,1,0:T(8,128)(2,1)}, u32[]{:S(2)}, u32[]{:S(2)}) %all-to-all-start) | async-done | bytes 9437216 | tf_op jit(solution)/shard_map/all_to_all | solution.py:16
  149.8 23.7 %copy.8 = bf16[64,2,24,4,384]{4,3,2,1,0:T(4,128)(2,1)} copy(bf16[64,2,24,4,384]{4,2,1,0,3:T(8,128)(2,1)} %bitcast.1) | data formatting | bytes 18874368 | tf_op jit(solution)/shard_map/reshape | solution.py:15
  173.5 9.0 copy.14
  182.4 7.8 fusion.3
  190.3 0.0 all-reduce.2.cloned.1.call-update
  190.3 0.0 all-gather.2.cloned.1.call-start
  190.3 0.0 reduce-scatter.3.cloned.1.call-done
  190.4 2.0 convert_element_type.6
  192.3 0.0 all-gather.2.cloned.1.call-update
  192.3 0.0 reduce-scatter.5.cloned.1.call-start
  192.4 0.0 copy-done.4
  192.4 5.5 convolution_bitcast_fusion
  197.9 10.5 %copy.9 = f32[16,2,256,256]{3,0,1,2:T(8,128)} copy(f32[16,2,256,256]{2,3,1,0:T(8,128)} %convolution_bitcast_fusion) | data formatting | bytes 16777216 | tf_op jit(solution)/shard_map/akjr,js->aksr/transpose | solution.py:42
  208.4 0.0 reduce-scatter.5.cloned.1.call-update
  208.4 0.0 copy-start.3
  208.4 691.0 %all-reduce.2.cloned.1.call-done = f32[384,1536]{1,0:T(8,128)} async-done(((f32[384,1536]{1,0:T(8,128)}), f32[384,1536]{1,0:T(8,128)}) %all-reduce.2.cloned.1.call-update) | async-done | bytes 2359312 | tf_op jit(solution)/shard_map/psum | solution.py:34
  899.4 3.3 broadcast_multiply_fusion
  902.7 4.5 convolution_bitcast_fusion.1
  907.2 55.5 %psum.15 = f32[24,384]{1,0:T(8,128)S(1)} all-reduce(f32[24,384]{1,0:T(8,128)S(1)} %convolution_bitcast_fusion.1), channel_id=1, replica_groups=mesh['gx'=4,'gy'=16,'gz'=4] {'gx','gz'}, use_global_device_ids=true, to_apply=%region_2.0 | all-reduce | flops 9216 | bytes 73728 | tf_op jit(solution)/shard_map/psum | solution.py:48
  962.7 0.6 broadcast_multiply_fusion.1
  963.4 1.1 convert_element_type.7
  964.4 0.9 copy.10
  965.3 0.0 copy-done.1
  (6 shorter events, 0.0 us)
Async XLA Ops:
  8.0 12.2 %copy-start = (bf16[384,256]{1,0:T(8,128)(2,1)S(1)}, bf16[384,256]{1,0:T(8,128)(2,1)}, u32[]{:S(2)}) copy-start(bf16[384,256]{1,0:T(8,128)(2,1)} %param.4) | copy-start | bytes 589828
  14.2 6.0 copy-start.2
  14.2 135.6 %all-to-all-start = ((bf16[4,64,2,24,384]{4,3,2,1,0:T(8,128)(2,1)}), bf16[4,64,2,24,384]{4,3,2,1,0:T(8,128)(2,1)}, u32[]{:S(2)}, u32[]{:S(2)}) async-start(bf16[4,64,2,24,384]{4,3,2,1,0:T(8,128)(2,1)} %stack.2), calls=%async_computation | async-start | bytes 18874368 | tf_op jit(solution)/shard_map/all_to_all | solution.py:16
  20.1 170.2 %reduce-scatter.3.cloned.1.call-start = ((), (), s32[]{:S(2)}) async-start(), calls=%async_computation.4 | async-start | bytes 3932160 | tf_op jit(solution)/shard_map/reduce_scatter | solution.py:28
  22.9 876.5 %all-reduce.2.cloned.1.call-start = ((), (), s32[]{:S(2)}) async-start(), calls=%async_computation.3 | async-start | bytes 4718592 | tf_op jit(solution)/shard_map/psum | solution.py:34
  190.3 2.1 copy-start.4
  190.3 712.4 %all-gather.2.cloned.1.call-start = ((), (), s32[]{:S(2)}) async-start(), calls=%async_computation.5 | async-start | bytes 6684672 | tf_op jit(solution)/shard_map/all_gather | solution.py:39
  192.3 771.0 %reduce-scatter.5.cloned.1.call-start = ((), (), s32[]{:S(2)}) async-start(), calls=%async_computation.6 | async-start | bytes 8912896 | tf_op jit(solution)/shard_map/reduce_scatter | solution.py:45
  208.4 694.3 %copy-start.3 = (bf16[16,2,24,256]{3,2,1,0:T(8,128)(2,1)S(1)}, bf16[16,2,24,256]{3,2,1,0:T(8,128)(2,1)}, u32[]{:S(2)}) copy-start(bf16[16,2,24,256]{3,2,1,0:T(8,128)(2,1)} %convert_element_type.6) | copy-start | bytes 1179652
  899.4 65.9 %copy-start.1 = (bf16[384,256]{1,0:T(8,128)(2,1)S(1)}, bf16[384,256]{1,0:T(8,128)(2,1)}, u32[]{:S(2)}) copy-start(bf16[384,256]{1,0:T(8,128)(2,1)} %param.4) | copy-start | bytes 589828
Sparse Core Ops, SparseCore 0:
  23.5 68.1 reduce-scatter.2
  193.7 119.0 all-gather.1
  316.9 222.9 reduce-scatter.4
Sparse Core Ops, SparseCore 1:
  190.4 709.0 all-reduce.1
